TPU v7x, 32 devices: a whole 2x2x4 slice. The times are simulated.
32 devices in a mesh: rep: 4 (over y, core), seq: 2 (over x), ctx: 4 (over z).
Axes of the slice: x: 2, y: 2, z: 4, core: 2. Of those that a mesh axis runs over, the one named last changes fastest.
Arguments:
- tokens: bfloat16 [8192, 2048], P(('rep', 'seq', 'ctx')), may hold values from -6 to 6
- cotangent: bfloat16 [8192, 2048], P(('rep', 'seq', 'ctx')), may hold values from -6 to 6
- document_index: int32 [8192], P(('rep', 'seq')), may hold values from 0 to 10, as said below
- padding_token_mask: int32 [8192], P(('rep', 'seq')), may hold values from 0 to 1, as said below
- attention_gain: bfloat16 [2048], P(('seq', 'ctx')), may hold values from 0.099609375 to 1.8984375
- projection_weight: bfloat16 [2048, 6144], P(('seq', 'ctx')), may hold values from -0.125 to 0.125
- head_gain: bfloat16 [2, 128], replicated, may hold values from 0.099609375 to 1.8984375
- out_weight: bfloat16 [2048, 2048], P(('seq', 'ctx')), may hold values from -2 to 2
- feedforward_gain: bfloat16 [2048], P(('seq', 'ctx')), may hold values from 0.099609375 to 1.8984375
- gate_weight: bfloat16 [2048, 6144], P(('seq', 'ctx')), may hold values from -0.125 to 0.125
- up_weight: bfloat16 [2048, 6144], P(('seq', 'ctx')), may hold values from -0.125 to 0.125
- down_weight: bfloat16 [2048, 6144], P(('seq', 'ctx')), may hold values from -0.078125 to 0.078125
Outputs:
- layer_out: bfloat16 [8192, 2048], P(('rep', 'seq', 'ctx'))
- tokens_grad: bfloat16 [8192, 2048], P(('rep', 'seq', 'ctx'))
- attention_gain_grad: float32 [2048], P(('seq', 'ctx'))
- proj_weight_grad: float32 [2048, 6144], P(('seq', 'ctx'))
- head_gain_grad: float32 [2, 128], replicated
- out_weight_grad: float32 [2048, 2048], P(('seq', 'ctx'))
- feedforward_gain_grad: float32 [2048], P(('seq', 'ctx'))
- gate_weight_grad: float32 [2048, 6144], P(('seq', 'ctx'))
- up_weight_grad: float32 [2048, 6144], P(('seq', 'ctx'))
- down_weight_grad: float32 [2048, 6144], P(('seq', 'ctx'))
Inputs may be any that keep to these rules, and one draw needn't show every extreme that they name: `document_index`: along each sequence of 1024 tokens the ids never fall. `padding_token_mask`: the zeros of a sequence form one run at its end.
All inputs are finite; a program needn't handle non-finite values.
Results may differ from a plain program's by a relative error of at most 0.02.
Values may be sent and summed in bfloat16 or wider, within the bound.
A program may use at most 640 MiB of HBM per device.

v0:
```python
import jax
import jax.numpy as jnp
from jax import lax
from jax.sharding import PartitionSpec as P

QUERY_HEADS = 16
KEY_VALUE_HEADS = 8
HEAD_SIZE = 128
norm_epsilon = 1e-06
rope_base = 1000000.0
masked_value = -1e30
contract_rows = (((0,), (0,)), ((), ()))
contract_cols = (((1,), (1,)), ((), ()))


def rope_tables(positions):
    half_size = HEAD_SIZE // 2
    frequency = rope_base ** (-2.0 * jnp.arange(half_size, dtype=jnp.float32) / HEAD_SIZE)
    angles = positions.astype(jnp.float32)[:, None, None] * frequency[None, None, :]
    return (jnp.cos(angles), jnp.sin(angles))


def rotate(value_rows, cosine_table, sine_table):
    half_size = value_rows.shape[-1] // 2
    first_half = value_rows[..., :half_size]
    second_half = value_rows[..., half_size:]
    return jnp.concatenate(
        [
            first_half * cosine_table - second_half * sine_table,
            second_half * cosine_table + first_half * sine_table,
        ],
        axis=-1,
    )


def inverse_rotation(grads, cosine_table, sine_table):
    half_size = grads.shape[-1] // 2
    first_half = grads[..., :half_size]
    second_half = grads[..., half_size:]
    return jnp.concatenate(
        [
            first_half * cosine_table + second_half * sine_table,
            second_half * cosine_table - first_half * sine_table,
        ],
        axis=-1,
    )


def head_norm(value_rows, gain):
    root_factor = lax.rsqrt(
        jnp.mean(value_rows * value_rows, axis=-1, keepdims=True) + norm_epsilon
    )
    unit_values = value_rows * root_factor
    return (unit_values * gain, unit_values, root_factor)


def norm_back(grad_out, unit_values, root_factor, gain):
    scaled = grad_out * gain
    return root_factor * (
        scaled - unit_values * jnp.mean(scaled * unit_values, axis=-1, keepdims=True)
    )


def over_replicas(grad_parts):
    return (
        lax.psum(grad_parts[0].astype(jnp.bfloat16), "rep").astype(jnp.float32),
        lax.psum(grad_parts[1].astype(jnp.bfloat16), "rep").astype(jnp.float32),
    )


def per_device(
    tokens,
    cotangent,
    document_index,
    padding_token_mask,
    attention_gain,
    projection_weight,
    head_gain,
    out_weight,
    feedforward_gain,
    gate_weight,
    up_weight,
    down_weight,
):
    token_rows = tokens.shape[0]
    sequence_length = document_index.shape[0]
    shard_rows = projection_weight.shape[0]
    proj_width = projection_weight.shape[1]
    ff_width = gate_weight.shape[1]
    query_total_width = QUERY_HEADS * HEAD_SIZE
    key_total_width = KEY_VALUE_HEADS * HEAD_SIZE
    query_group_width = QUERY_HEADS // KEY_VALUE_HEADS
    score_scale = HEAD_SIZE ** (-0.5)
    tokens_wide = tokens.astype(jnp.float32)
    root_attn = lax.rsqrt(jnp.mean(tokens_wide * tokens_wide, axis=1, keepdims=True) + norm_epsilon)
    unit_attn = tokens_wide * root_attn
    gain_piece = lax.all_gather(attention_gain, ("seq", "ctx"), axis=0, tiled=True)
    weight_piece = lax.all_gather(projection_weight, ("seq", "ctx"), axis=0, tiled=True)
    columns = unit_attn
    normed = (columns * gain_piece.astype(jnp.float32)).astype(jnp.bfloat16)
    result = (
        jnp.dot(normed, weight_piece, preferred_element_type=jnp.float32),
        gain_piece.astype(jnp.float32),
        normed,
    )
    folded_proj = result
    projected_rows = folded_proj[0]
    gain_attn_full = folded_proj[1]
    normed_attn = folded_proj[2]
    queries_raw = projected_rows[:, :query_total_width].reshape(token_rows, QUERY_HEADS, HEAD_SIZE)
    gate_logits = projected_rows[:, query_total_width : 2 * query_total_width]
    keys_raw = projected_rows[
        :, 2 * query_total_width : 2 * query_total_width + key_total_width
    ].reshape(token_rows, KEY_VALUE_HEADS, HEAD_SIZE)
    values_raw = projected_rows[:, 2 * query_total_width + key_total_width :]
    first_row = lax.axis_index("ctx") * token_rows
    positions = first_row + jnp.arange(token_rows, dtype=jnp.int32)
    cosine_table, sine_table = rope_tables(positions)
    head_gain_wide = head_gain.astype(jnp.float32)
    query_normed, query_unit, query_root = head_norm(queries_raw, head_gain_wide[0])
    key_normed, key_unit, key_root = head_norm(keys_raw, head_gain_wide[1])
    query_low = (
        rotate(query_normed, cosine_table, sine_table)
        .astype(jnp.bfloat16)
        .reshape(token_rows, KEY_VALUE_HEADS, query_group_width, HEAD_SIZE)
    )
    key_low = (
        rotate(key_normed, cosine_table, sine_table)
        .astype(jnp.bfloat16)
        .reshape(token_rows, key_total_width)
    )
    value_low = values_raw.astype(jnp.bfloat16)
    every_key, every_value = (
        lax.all_gather(key_low, "ctx", axis=0, tiled=True),
        lax.all_gather(value_low, "ctx", axis=0, tiled=True),
    )
    every_key = every_key.reshape(sequence_length, KEY_VALUE_HEADS, HEAD_SIZE)
    every_value = every_value.reshape(sequence_length, KEY_VALUE_HEADS, HEAD_SIZE)
    seg_here = lax.dynamic_slice_in_dim(document_index, first_row, token_rows, 0)
    pad_here = lax.dynamic_slice_in_dim(padding_token_mask, first_row, token_rows, 0)
    key_places = jnp.arange(sequence_length, dtype=jnp.int32)
    allowed = (seg_here[:, None] == document_index[None, :]) & (
        key_places[None, :] <= positions[:, None]
    ) & (padding_token_mask[None, :] == 1) | (key_places[None, :] == positions[:, None])

    def masked_scores():
        raw_scores = (
            jnp.einsum("qhgd,khd->hgqk", query_low, every_key, preferred_element_type=jnp.float32)
            * score_scale
        )
        return jnp.where(allowed[None, None], raw_scores, masked_value)

    scores = masked_scores()
    peak = jnp.max(scores, axis=3, keepdims=True)
    exp_scores = jnp.exp(scores - peak)
    denominator = jnp.sum(exp_scores, axis=3, keepdims=True)
    log_total = peak + jnp.log(denominator)
    probs_low = (exp_scores / denominator).astype(jnp.bfloat16)
    attended_rows = jnp.einsum(
        "hgqk,khd->qhgd", probs_low, every_value, preferred_element_type=jnp.float32
    ).reshape(token_rows, query_total_width)
    gate_activations = jax.nn.sigmoid(gate_logits)
    mixed_heads = (attended_rows * gate_activations).astype(jnp.bfloat16)
    columns = lax.dot_general(
        mixed_heads,
        lax.all_gather(out_weight, ("seq", "ctx"), axis=0, tiled=True),
        contract_cols,
        preferred_element_type=jnp.float32,
    )
    result = (columns,)
    folded_out = result
    resid_mid = tokens_wide + folded_out[0]
    root_mlp = lax.rsqrt(jnp.mean(resid_mid * resid_mid, axis=1, keepdims=True) + norm_epsilon)
    unit_mlp = resid_mid * root_mlp
    gain_piece = lax.all_gather(feedforward_gain, ("seq", "ctx"), axis=0, tiled=True)
    gate_piece = lax.all_gather(gate_weight, ("seq", "ctx"), axis=0, tiled=True)
    up_piece = lax.all_gather(up_weight, ("seq", "ctx"), axis=0, tiled=True)
    columns = unit_mlp
    normed = (columns * gain_piece.astype(jnp.float32)).astype(jnp.bfloat16)
    result = (
        jnp.dot(normed, gate_piece, preferred_element_type=jnp.float32),
        jnp.dot(normed, up_piece, preferred_element_type=jnp.float32),
        gain_piece.astype(jnp.float32),
        normed,
    )
    folded_mlp = result
    gate_lin = folded_mlp[0]
    up_lin = folded_mlp[1]
    gain_mlp_full = folded_mlp[2]
    normed_mlp = folded_mlp[3]
    gate_sig = jax.nn.sigmoid(gate_lin)
    silu_gate = gate_lin * gate_sig
    hidden_low = (silu_gate * up_lin).astype(jnp.bfloat16)
    columns = lax.dot_general(
        hidden_low,
        lax.all_gather(down_weight, ("seq", "ctx"), axis=0, tiled=True),
        contract_cols,
        preferred_element_type=jnp.float32,
    )
    result = (columns,)
    layer_out = (resid_mid + result[0]).astype(jnp.bfloat16)
    masked_grad = cotangent.astype(jnp.float32) * pad_here.astype(jnp.float32)[:, None]
    d_out_low = masked_grad.astype(jnp.bfloat16)
    columns = d_out_low
    d_hidden = jnp.dot(
        columns,
        lax.all_gather(down_weight, ("seq", "ctx"), axis=0, tiled=True),
        preferred_element_type=jnp.float32,
    )
    d_gate_low = (d_hidden * up_lin * gate_sig * (1.0 + gate_lin * (1.0 - gate_sig))).astype(
        jnp.bfloat16
    )
    d_up_low = (d_hidden * silu_gate).astype(jnp.bfloat16)
    gate_piece = lax.all_gather(gate_weight, ("seq", "ctx"), axis=0, tiled=True)
    up_piece = lax.all_gather(up_weight, ("seq", "ctx"), axis=0, tiled=True)
    columns = lax.dot_general(
        d_gate_low, gate_piece, contract_cols, preferred_element_type=jnp.float32
    ) + lax.dot_general(d_up_low, up_piece, contract_cols, preferred_element_type=jnp.float32)
    d_normed_mlp = columns
    normed_rows = normed_mlp
    grad_rows = d_out_low
    mlp_grads = lax.psum_scatter(
        jnp.concatenate(
            [
                lax.dot_general(
                    normed_rows, d_gate_low, contract_rows, preferred_element_type=jnp.float32
                ),
                lax.dot_general(
                    normed_rows, d_up_low, contract_rows, preferred_element_type=jnp.float32
                ),
                lax.dot_general(
                    grad_rows, hidden_low, contract_rows, preferred_element_type=jnp.float32
                ),
            ],
            axis=1,
        ).astype(jnp.bfloat16),
        ("seq", "ctx"),
        scatter_dimension=0,
        tiled=True,
    ).astype(jnp.float32)
    gain_mlp_term = jnp.sum(d_normed_mlp * unit_mlp, axis=0)
    d_resid_mid = masked_grad + norm_back(d_normed_mlp, unit_mlp, root_mlp, gain_mlp_full)
    d_attn_low = d_resid_mid.astype(jnp.bfloat16)
    columns = d_attn_low
    mixed_gradient = jnp.dot(
        columns,
        lax.all_gather(out_weight, ("seq", "ctx"), axis=0, tiled=True),
        preferred_element_type=jnp.float32,
    )
    d_gate_logits = mixed_gradient * attended_rows * gate_activations * (1.0 - gate_activations)
    d_attended_low = (
        (mixed_gradient * gate_activations)
        .astype(jnp.bfloat16)
        .reshape(token_rows, KEY_VALUE_HEADS, query_group_width, HEAD_SIZE)
    )
    probs = jnp.exp(masked_scores() - log_total)
    d_probs = jnp.einsum(
        "qhgd,khd->hgqk", d_attended_low, every_value, preferred_element_type=jnp.float32
    )
    value_term = jnp.einsum(
        "hgqk,qhgd->khd", probs_low, d_attended_low, preferred_element_type=jnp.float32
    )
    delta = jnp.sum(probs * d_probs, axis=3, keepdims=True)
    d_scores_low = (probs * (d_probs - delta)).astype(jnp.bfloat16)
    d_queries = (
        jnp.einsum("hgqk,khd->qhgd", d_scores_low, every_key, preferred_element_type=jnp.float32)
        * score_scale
    )
    key_term = (
        jnp.einsum("hgqk,qhgd->khd", d_scores_low, query_low, preferred_element_type=jnp.float32)
        * score_scale
    )
    key_gradient, d_values = (
        lax.psum_scatter(
            key_term.reshape(sequence_length, key_total_width).astype(jnp.bfloat16),
            "ctx",
            scatter_dimension=0,
            tiled=True,
        ).astype(jnp.float32),
        lax.psum_scatter(
            value_term.reshape(sequence_length, key_total_width).astype(jnp.bfloat16),
            "ctx",
            scatter_dimension=0,
            tiled=True,
        ).astype(jnp.float32),
    )
    d_query_normed = inverse_rotation(
        d_queries.reshape(token_rows, QUERY_HEADS, HEAD_SIZE), cosine_table, sine_table
    )
    normed_key_gradient = inverse_rotation(
        key_gradient.reshape(token_rows, KEY_VALUE_HEADS, HEAD_SIZE), cosine_table, sine_table
    )
    head_term = jnp.stack(
        [
            jnp.sum(d_query_normed * query_unit, axis=(0, 1)),
            jnp.sum(normed_key_gradient * key_unit, axis=(0, 1)),
        ]
    )
    d_query_raw = norm_back(d_query_normed, query_unit, query_root, head_gain_wide[0])
    d_key_raw = norm_back(normed_key_gradient, key_unit, key_root, head_gain_wide[1])
    d_proj_low = jnp.concatenate(
        [
            d_query_raw.reshape(token_rows, query_total_width),
            d_gate_logits,
            d_key_raw.reshape(token_rows, key_total_width),
            d_values,
        ],
        axis=1,
    ).astype(jnp.bfloat16)
    columns = lax.dot_general(
        d_proj_low,
        lax.all_gather(projection_weight, ("seq", "ctx"), axis=0, tiled=True),
        contract_cols,
        preferred_element_type=jnp.float32,
    )
    normed_rows = normed_attn
    grad_rows = d_attn_low
    attn_grads = lax.psum_scatter(
        jnp.concatenate(
            [
                lax.dot_general(
                    normed_rows, d_proj_low, contract_rows, preferred_element_type=jnp.float32
                ),
                lax.dot_general(
                    grad_rows, mixed_heads, contract_rows, preferred_element_type=jnp.float32
                ),
            ],
            axis=1,
        ).astype(jnp.bfloat16),
        ("seq", "ctx"),
        scatter_dimension=0,
        tiled=True,
    ).astype(jnp.float32)
    gain_attn_term = jnp.sum(columns * unit_attn, axis=0)
    tokens_grad = (d_resid_mid + norm_back(columns, unit_attn, root_attn, gain_attn_full)).astype(
        jnp.bfloat16
    )
    sum_attn_gain, sum_mlp_gain, sum_head_gain = lax.psum(
        (gain_attn_term, gain_mlp_term, head_term), ("rep", "seq", "ctx")
    )
    mlp_grads, attn_grads = over_replicas((mlp_grads, attn_grads))
    group_rank = lax.axis_index(("seq", "ctx"))
    attention_gain_grad = lax.dynamic_slice_in_dim(
        sum_attn_gain, group_rank * shard_rows, shard_rows, 0
    )
    feedforward_gain_grad = lax.dynamic_slice_in_dim(
        sum_mlp_gain, group_rank * shard_rows, shard_rows, 0
    )
    return (
        layer_out,
        tokens_grad,
        attention_gain_grad,
        attn_grads[:, :proj_width],
        sum_head_gain,
        attn_grads[:, proj_width:],
        feedforward_gain_grad,
        mlp_grads[:, :ff_width],
        mlp_grads[:, ff_width : 2 * ff_width],
        mlp_grads[:, 2 * ff_width :],
    )


def solution(mesh):
    in_specs = (
        P(("rep", "seq", "ctx"), None),
        P(("rep", "seq", "ctx"), None),
        P(("rep", "seq")),
        P(("rep", "seq")),
        P(("seq", "ctx")),
        P(("seq", "ctx"), None),
        P(),
        P(("seq", "ctx"), None),
        P(("seq", "ctx")),
        P(("seq", "ctx"), None),
        P(("seq", "ctx"), None),
        P(("seq", "ctx"), None),
    )
    out_specs = (
        P(("rep", "seq", "ctx"), None),
        P(("rep", "seq", "ctx"), None),
        P(("seq", "ctx")),
        P(("seq", "ctx"), None),
        P(),
        P(("seq", "ctx"), None),
        P(("seq", "ctx")),
        P(("seq", "ctx"), None),
        P(("seq", "ctx"), None),
        P(("seq", "ctx"), None),
    )
    return jax.shard_map(
        per_device, mesh=mesh, in_specs=in_specs, out_specs=out_specs, check_vma=False
    )
```

profile of v0, /device:TPU:0, one launch (start us, length us, event | category | flops | bytes accessed | tf_op | source)
XLA Modules:
  0.0 4382.5 jit_solution(18146430784652032975)
XLA Ops:
  8.0 22.4 all-gather
  30.7 462.0 %all-gather.10.cloned.1.call-done = bf16[2048,6144]{1,0:T(8,128)(2,1)} async-done(((bf16[256,6144]{1,0:T(8,128)(2,1)}), bf16[2048,6144]{1,0:T(8,128)(2,1)}) %all-gather.10.cloned.1.call-update) | async-done | bytes 25165840 | tf_op jit(solution)/shard_map/all_gather | solution.py:98
  492.8 11.7 fusion.46
  504.5 2.7 copy-done.13
  508.8 1.4 slice_bitcast_fusion.1
  516.4 20.9 all-gather.1
  538.3 1.7 slice_bitcast_fusion
  545.0 10.4 all-gather.12.cloned.1.call-done
  555.5 2.2 copy.123
  557.7 45.0 %all-gather.14.cloned.1.call-done = bf16[1024,1024]{0,1:T(8,128)(2,1)} async-done(((bf16[256,1024]{0,1:T(8,128)(2,1)}), bf16[1024,1024]{0,1:T(8,128)(2,1)}) %all-gather.14.cloned.1.call-update) | async-done | bytes 2097168 | tf_op jit(solution)/shard_map/all_gather | solution.py:134
  602.7 12.2 fusion.56
  615.0 8.1 fusion.3
  623.1 7.6 divide_convert_fusion
  630.7 3.2 fusion.27
  634.7 1.9 copy.113
  636.6 3.9 multiply_convert_fusion.6
  640.5 87.4 %all-gather.16.cloned.1.call-done = bf16[2048,2048]{1,0:T(8,128)(2,1)} async-done(((bf16[256,2048]{1,0:T(8,128)(2,1)}), bf16[2048,2048]{1,0:T(8,128)(2,1)}) %all-gather.16.cloned.1.call-update) | async-done | bytes 8388624 | tf_op jit(solution)/shard_map/all_gather | solution.py:166
  727.9 6.2 multiply_reduce_fusion.3
  734.4 473.5 %all-gather.18.cloned.1.call-done = bf16[2048,6144]{1,0:T(8,128)(2,1)} async-done(((bf16[256,6144]{1,0:T(8,128)(2,1)}), bf16[2048,6144]{1,0:T(8,128)(2,1)}) %all-gather.18.cloned.1.call-update) | async-done | bytes 25165840 | tf_op jit(solution)/shard_map/all_gather | solution.py:176
  1207.9 14.3 fusion.57
  1222.2 468.7 %all-gather.20.cloned.1.call-done = bf16[2048,6144]{1,0:T(8,128)(2,1)} async-done(((bf16[256,6144]{1,0:T(8,128)(2,1)}), bf16[2048,6144]{1,0:T(8,128)(2,1)}) %all-gather.20.cloned.1.call-update) | async-done | bytes 25165840 | tf_op jit(solution)/shard_map/all_gather | solution.py:177
  1690.9 14.3 fusion.58
  1705.3 468.9 %all-gather.22.cloned.1.call-done = bf16[2048,6144]{1,0:T(8,128)(2,1)} async-done(((bf16[256,6144]{1,0:T(8,128)(2,1)}), bf16[2048,6144]{1,0:T(8,128)(2,1)}) %all-gather.22.cloned.1.call-update) | async-done | bytes 25165840 | tf_op jit(solution)/shard_map/all_gather | solution.py:196
  2174.1 19.1 multiply_convert_fusion
  2193.2 13.5 fusion.59
  2206.7 15.2 multiply_reduce_fusion
  2221.9 2.4 multiply_add_fusion.1
  2224.4 8.6 multiply_convert_fusion.3
  2234.1 14.6 fusion
  2251.1 10.1 fusion.2
  2261.3 7.7 fusion.5
  2270.3 7.5 bitcast_convert_fusion
  2277.8 4.1 copy.117
  2282.0 4.7 convolution_multiply_fusion
  2287.9 2.6 copy.119
  2290.5 2.5 copy.118
  2293.0 2.2 multiply_add_fusion
  2295.2 2.1 multiply_reduce_fusion.1
  2298.6 4.8 fusion.22
  2303.4 5.7 convolution_convert_fusion.4
  2309.1 5.0 reduce-scatter.5.cloned.1.call-done
  2314.1 1.9 fusion.55
  2316.4 2.5 copy.120
  2318.9 1.4 multiply_add_fusion.2
  2320.4 1.6 multiply_reduce_fusion.5
  2322.7 2.7 fusion.34
  2325.4 34.5 reduce-scatter.7.cloned.1.call-done
  2359.9 12.6 convolution_convert_fusion.3
  2372.5 22.9 pad_maximum_fusion.1
  2396.6 13.9 convolution_convert_fusion.1
  2410.5 14.0 convolution_convert_fusion.2
  2424.5 14.2 convolution_convert_fusion
  2438.7 50.8 %pad_maximum_fusion = bf16[2048,18432]{1,0:T(8,128)(2,1)} fusion(bf16[2048,6144]{1,0:T(8,128)(2,1)} %convolution_convert_fusion, bf16[2048,6144]{1,0:T(8,128)(2,1)} %convolution_convert_fusion.1, bf16[2048,6144]{1,0:T(8,128)(2,1)} %convolution_convert_fusion.2), kind=kLoop, calls=%fused_computation | loop fusion | flops 226492416 | bytes 150994944 | tf_op jit(solution)/shard_map/concatenate | solution.py:223
  2489.5 448.2 %reduce-scatter.9.cloned.1.call-done = bf16[256,8192]{1,0:T(8,128)(2,1)} async-done(((bf16[2048,8192]{1,0:T(8,128)(2,1)}), bf16[256,8192]{1,0:T(8,128)(2,1)}) %reduce-scatter.9.cloned.1.call-update) | async-done | bytes 4194320 | tf_op jit(solution)/shard_map/reduce_scatter | solution.py:318
  2937.7 1180.7 %reduce-scatter.11.cloned.1.call-done = bf16[256,18432]{1,0:T(8,128)(2,1)} async-done(((bf16[2048,18432]{1,0:T(8,128)(2,1)}), bf16[256,18432]{1,0:T(8,128)(2,1)}) %reduce-scatter.11.cloned.1.call-update) | async-done | bytes 9437200 | tf_op jit(solution)/shard_map/reduce_scatter | solution.py:222
  4118.5 1.5 copy-done.20
  4120.0 15.0 fusion.10
  4135.1 14.9 fusion.17
  4150.0 40.8 all-reduce
  4192.0 3.2 fusion.16
  4195.1 164.5 %all-reduce.4.cloned.1.call-done = (bf16[256,8192]{1,0:T(8,128)(2,1)}, bf16[256,18432]{1,0:T(8,128)(2,1)}) async-done(((bf16[256,8192]{1,0:T(8,128)(2,1)}, bf16[256,18432]{1,0:T(8,128)(2,1)}), (bf16[256,8192]{1,0:T(8,128)(2,1)}, bf16[256,18432]{1,0:T(8,128)(2,1)})) %all-reduce.4.cloned.1.call-update) | async-done | bytes 13631504 | tf_op jit(solution)/shard_map/psum | solution.py:67
  4359.7 5.9 slice.91
  4365.6 2.8 slice.92
  4368.4 6.9 fusion.53
  (197 shorter events, 26.6 us)
Async XLA Ops:
  7.2 23.2 copy-start.16
  7.2 485.6 %all-gather.10.cloned.1.call-start = ((), (), s32[]{:S(2)}) async-start(), calls=%async_computation.4 | async-start | bytes 28311552 | tf_op jit(solution)/shard_map/all_gather | solution.py:98
  7.9 547.5 %all-gather.12.cloned.1.call-start = ((), (), s32[]{:S(2)}) async-start(), calls=%async_computation.5 | async-start | bytes 2621440 | tf_op jit(solution)/shard_map/all_gather | solution.py:135
  30.4 474.1 %copy-start.36 = (f32[8,1,256]{2,1,0:T(1,128)}, f32[8,1,256]{2,1,0:T(1,128)S(1)}, u32[]{:S(2)}) copy-start(f32[8,1,256]{2,1,0:T(1,128)S(1)} %convert_element_type.136) | copy-start | bytes 24580
  30.7 473.8 %copy-start.38 = (f32[256]{0:T(256)}, f32[256]{0:T(256)S(1)}, u32[]{:S(2)}) copy-start(f32[256]{0:T(256)S(1)} %add_rsqrt_fusion.3) | copy-start | bytes 3076
  492.8 15.4 copy-start.55
  504.5 2.7 copy-start.13
  508.1 94.6 %all-gather.14.cloned.1.call-start = ((), (), s32[]{:S(2)}) async-start(), calls=%async_computation.6 | async-start | bytes 2621440 | tf_op jit(solution)/shard_map/all_gather | solution.py:134
  508.2 3.6 copy-start.47
  508.2 32.9 copy-start.49
  508.8 33.9 copy-start.27
  508.8 33.9 copy-start.29
  513.8 214.1 %all-gather.16.cloned.1.call-start = ((), (), s32[]{:S(2)}) async-start(), calls=%async_computation.7 | async-start | bytes 9437184 | tf_op jit(solution)/shard_map/all_gather | solution.py:166
  514.4 693.5 %all-gather.18.cloned.1.call-start = ((), (), s32[]{:S(2)}) async-start(), calls=%async_computation.8 | async-start | bytes 28311552 | tf_op jit(solution)/shard_map/all_gather | solution.py:176
  515.0 22.3 copy-start.52
  515.0 22.4 copy-start.53
  515.0 1175.9 %all-gather.20.cloned.1.call-start = ((), (), s32[]{:S(2)}) async-start(), calls=%async_computation.9 | async-start | bytes 28311552 | tf_op jit(solution)/shard_map/all_gather | solution.py:177
  515.6 1658.5 %all-gather.22.cloned.1.call-start = ((), (), s32[]{:S(2)}) async-start(), calls=%async_computation.10 | async-start | bytes 28311552 | tf_op jit(solution)/shard_map/all_gather | solution.py:196
  516.3 1797.7 %reduce-scatter.5.cloned.1.call-start = ((), (), s32[]{:S(2)}) async-start(), calls=%async_computation.11 | async-start | bytes 2621440 | tf_op jit(solution)/shard_map/reduce_scatter | solution.py:274
  541.1 2.4 copy-start.32
  543.7 59.0 %copy-start.14 = (bf16[256,16,64]{2,0,1:T(8,128)(2,1)}, bf16[256,16,64]{2,0,1:T(8,128)(2,1)S(1)}, u32[]{:S(2)}) copy-start(bf16[256,16,64]{2,0,1:T(8,128)(2,1)S(1)} %copy.80) | copy-start | bytes 1572868
  557.7 73.0 %copy-start.7 = (bf16[128,8,8,128]{3,2,1,0:T(8,128)(2,1)}, bf16[128,8,8,128]{3,2,1,0:T(8,128)(2,1)S(1)}, u32[]{:S(2)}) copy-start(bf16[128,8,8,128]{3,2,1,0:T(8,128)(2,1)S(1)} %copy.123) | copy-start | bytes 6291460
  615.0 8.1 copy-start.40
  623.1 7.7 copy-start.42
  630.7 4.0 copy-start
  636.6 3.9 copy-start.21
  636.6 91.3 %copy-start.17 = (bf16[256,2048]{1,0:T(8,128)(2,1)S(1)}, bf16[256,2048]{1,0:T(8,128)(2,1)}, u32[]{:S(2)}) copy-start(bf16[256,2048]{1,0:T(8,128)(2,1)} %param.12) | copy-start | bytes 3145732
  734.1 1487.8 %copy-start.19 = (f32[256,2048]{1,0:T(8,128)}, f32[256,2048]{1,0:T(8,128)S(1)}, u32[]{:S(2)}) copy-start(f32[256,2048]{1,0:T(8,128)S(1)} %get-tuple-element.54) | copy-start | bytes 6291460
  734.4 956.6 %copy-start.11 = (bf16[256,2048]{1,0:T(8,128)(2,1)}, bf16[256,2048]{1,0:T(8,128)(2,1)S(1)}, u32[]{:S(2)}) copy-start(bf16[256,2048]{1,0:T(8,128)(2,1)S(1)} %multiply_convert_fusion.5) | copy-start | bytes 3145732
  2206.7 15.2 copy-start.23
  2221.9 2.4 copy-start.22
  2224.3 8.6 copy-start.4
  2224.3 9.1 copy-start.41
  2224.3 9.1 copy-start.43
  2234.1 14.7 slice-start
  2234.1 14.7 slice-start.1
  2234.1 15.9 slice-start.2
  2234.1 17.1 slice-start.3
  2251.1 10.1 copy-start.15
  2261.3 7.8 copy-start.48
  2261.3 8.4 copy-start.50
  2269.0 90.8 %reduce-scatter.7.cloned.1.call-start = ((), (), s32[]{:S(2)}) async-start(), calls=%async_computation.12 | async-start | bytes 2621440 | tf_op jit(solution)/shard_map/reduce_scatter | solution.py:280
  2277.8 4.2 copy-start.8
  2281.9 655.8 %reduce-scatter.9.cloned.1.call-start = ((), (), s32[]{:S(2)}) async-start(), calls=%async_computation.13 | async-start | bytes 37748736 | tf_op jit(solution)/shard_map/reduce_scatter | solution.py:318
  2287.9 5.1 copy-start.28
  2287.9 5.1 copy-start.30
  2292.9 2.3 copy-start.33
  2298.5 4.8 copy-start.5
  2298.6 4.8 copy-start.26
  2303.4 56.5 %copy-start.25 = (bf16[256,2048]{1,0:T(8,128)(2,1)}, bf16[256,2048]{1,0:T(8,128)(2,1)S(1)}, u32[]{:S(2)}) copy-start(bf16[256,2048]{1,0:T(8,128)(2,1)S(1)} %get-tuple-element.27) | copy-start | bytes 3145732
  2316.4 3.9 copy-start.10
  2316.4 3.9 copy-start.35
  2320.3 2.3 copy-start.46
  2322.3 37.6 copy-start.18
  2322.3 37.6 copy-start.37
  2322.3 37.6 copy-start.39
  2325.3 47.1 %copy-start.31 = (bf16[256,1024]{1,0:T(8,128)(2,1)}, bf16[256,1024]{1,0:T(8,128)(2,1)S(1)}, u32[]{:S(2)}) copy-start(bf16[256,1024]{1,0:T(8,128)(2,1)S(1)} %get-tuple-element.32) | copy-start | bytes 1572868
  2395.4 1723.1 %reduce-scatter.11.cloned.1.call-start = ((), (), s32[]{:S(2)}) async-start(), calls=%async_computation.14 | async-start | bytes 84934656 | tf_op jit(solution)/shard_map/reduce_scatter | solution.py:222
  2410.5 14.0 copy-start.24
  2489.5 1870.2 %all-reduce.4.cloned.1.call-start = ((), (), s32[]{:S(2)}) async-start(), calls=%async_computation.15 | async-start | bytes 27262976 | tf_op jit(solution)/shard_map/psum | solution.py:67
  4120.0 15.0 copy-start.45
  4135.1 14.9 copy-start.51
  4135.1 56.9 %copy-start.6 = (f32[256,2048]{1,0:T(8,128)S(1)}, f32[256,2048]{1,0:T(8,128)}, u32[]{:S(2)}) copy-start(f32[256,2048]{1,0:T(8,128)} %copy-done.4) | copy-start | bytes 6291460
  4359.7 8.7 copy-start.1
  (9 other events, 12.0 us)
Sparse Core Ops, SparseCore 0:
  9.6 483.1 all-gather.9
  508.2 47.1 all-gather.11
  557.6 45.0 all-gather.13
  604.7 123.1 all-gather.15
  729.3 478.5 all-gather.17
  1209.3 481.6 all-gather.19
  1692.5 481.6 all-gather.21
  2269.1 44.8 reduce-scatter.4
  2316.5 43.3 reduce-scatter.6
  2395.5 542.1 reduce-scatter.8
  2941.6 1176.8 reduce-scatter.10
  4121.1 238.5 all-reduce.3
where the time goes:
time: 4390 us; the launch traced here: 4380 us
  waiting for transfers between devices  3850 us (88%)
  matrix products  243 us (6%)
  other arithmetic  130 us (3%)
  blocking collectives  84 us (2%)
  local copies, waits for them, and re-layouts  57.2 us (1%)
    reduce_scatter x1, waiting for transfers between devices, per_device(): lax.psum_scatter(jnp.concatenate([lax.dot_general(normed_rows, d_gate_low...  1180 us
    all_gather x1, waiting for transfers between devices, per_device(): gate_piece = lax.all_gather(gate_weight, ('seq', 'ctx'), axis=0, tiled=True)  474 us
    all_gather x1, waiting for transfers between devices, per_device(): lax.all_gather(down_weight, ('seq', 'ctx'), axis=0, tiled=True)  469 us
    all_gather x1, waiting for transfers between devices, per_device(): up_piece = lax.all_gather(up_weight, ('seq', 'ctx'), axis=0, tiled=True)  469 us
    all_gather x1, waiting for transfers between devices, per_device(): lax.all_gather(projection_weight, ('seq', 'ctx'), axis=0, tiled=True)  462 us
    reduce_scatter x1, waiting for transfers between devices, per_device(): lax.psum_scatter(jnp.concatenate([lax.dot_general(normed_rows, d_proj_low...  448 us
    psum x1, waiting for transfers between devices, over_replicas(): lax.psum(grad_parts[1].astype(jnp.bfloat16), 'rep').astype(jnp.float32)  165 us
  transfers between devices with their start and end apart: 12, of which 12 were waited for; matrix products, arithmetic and copies ran while one was open for 6% of the time, Pallas kernels for 0%

commit v1 on v0

--- a/solution.py
+++ b/solution.py
@@ -173,8 +173,16 @@
     root_mlp = lax.rsqrt(jnp.mean(resid_mid * resid_mid, axis=1, keepdims=True) + norm_epsilon)
     unit_mlp = resid_mid * root_mlp
     gain_piece = lax.all_gather(feedforward_gain, ("seq", "ctx"), axis=0, tiled=True)
-    gate_piece = lax.all_gather(gate_weight, ("seq", "ctx"), axis=0, tiled=True)
-    up_piece = lax.all_gather(up_weight, ("seq", "ctx"), axis=0, tiled=True)
+
+    def supply_the_zones(target, mat):
+        r1 = jnp.concatenate([target, mat], axis=1)
+        return jnp.split(
+            lax.all_gather(r1, axis=0, axis_name=("seq", "ctx"), tiled=True),
+            [target.shape[1]],
+            axis=1,
+        )
+
+    gate_piece, up_piece = supply_the_zones(gate_weight, up_weight)
     columns = unit_mlp
     normed = (columns * gain_piece.astype(jnp.float32)).astype(jnp.bfloat16)
     result = (

time: 4390 us -> 5310 us (1.21)
  waiting for transfers between devices: 3850 us -> 4770 us
    all_gather x0 -> x1, waiting for transfers between devices: none -> 945 us  [supply_the_zones(): lax.all_gather(r1, axis=0, axis_name=('seq', 'ctx'), tiled=True)]
  transfers between devices with their start and end apart: 12 -> 13, of which waited for: 12 -> 13; matrix products, arithmetic and copies ran while one was open for 6% -> 6% of each run, Pallas kernels for 0% -> 0%
where the time goes in v1:
time: 5310 us; the launch traced here: 5300 us
  waiting for transfers between devices  4770 us (90%)
  matrix products  242 us (5%)
  other arithmetic  137 us (3%)
  blocking collectives  84.4 us (2%)
  local copies, waits for them, and re-layouts  58.2 us (1%)
    reduce_scatter x1, waiting for transfers between devices, per_device(): lax.psum_scatter(jnp.concatenate([lax.dot_general(normed_rows, d_gate_low...  1180 us
    all_gather x1, waiting for transfers between devices, supply_the_zones(): lax.all_gather(r1, axis=0, axis_name=('seq', 'ctx'), tiled=True)  945 us
    all_gather x1, waiting for transfers between devices, per_device(): up_piece = lax.all_gather(up_weight, ('seq', 'ctx'), axis=0, tiled=True)  470 us
    all_gather x1, waiting for transfers between devices, per_device(): gate_piece = lax.all_gather(gate_weight, ('seq', 'ctx'), axis=0, tiled=True)  463 us
    all_gather x1, waiting for transfers between devices, per_device(): lax.all_gather(projection_weight, ('seq', 'ctx'), axis=0, tiled=True)  462 us
    all_gather x1, waiting for transfers between devices, per_device(): lax.all_gather(down_weight, ('seq', 'ctx'), axis=0, tiled=True)  457 us
    reduce_scatter x1, waiting for transfers between devices, per_device(): lax.psum_scatter(jnp.concatenate([lax.dot_general(normed_rows, d_proj_low...  449 us
    psum x1, waiting for transfers between devices, over_replicas(): lax.psum(grad_parts[1].astype(jnp.bfloat16), 'rep').astype(jnp.float32)  165 us
  transfers between devices with their start and end apart: 13, of which 13 were waited for; matrix products, arithmetic and copies ran while one was open for 6% of the time, Pallas kernels for 0%

profile of v1, /device:TPU:0, one launch (start us, length us, event | category | flops | bytes accessed | tf_op | source)
XLA Modules:
  0.0 5304.8 jit_solution(2832167608420305301)
XLA Ops:
  8.0 22.4 all-gather
  30.7 462.0 %all-gather.11.cloned.1.call-done = bf16[2048,6144]{1,0:T(8,128)(2,1)} async-done(((bf16[256,6144]{1,0:T(8,128)(2,1)}), bf16[2048,6144]{1,0:T(8,128)(2,1)}) %all-gather.11.cloned.1.call-update) | async-done | bytes 25165840 | tf_op jit(solution)/shard_map/all_gather | solution.py:98
  492.8 11.7 fusion.50
  504.5 2.7 copy-done.13
  513.4 2.1 copy.78
  516.2 5.3 pad_maximum_fusion.2
  523.7 21.2 all-gather.1
  546.5 1.7 slice_bitcast_fusion
  553.3 2.2 all-gather.13.cloned.1.call-done
  555.5 2.2 copy.123
  557.7 44.9 all-gather.15.cloned.1.call-done
  602.7 12.2 fusion.60
  614.9 8.0 fusion.7
  622.9 7.6 divide_convert_fusion
  630.6 3.2 fusion.31
  634.5 1.9 copy.113
  636.5 3.9 multiply_convert_fusion.6
  640.4 87.5 %all-gather.17.cloned.1.call-done = bf16[2048,2048]{1,0:T(8,128)(2,1)} async-done(((bf16[256,2048]{1,0:T(8,128)(2,1)}), bf16[2048,2048]{1,0:T(8,128)(2,1)}) %all-gather.17.cloned.1.call-update) | async-done | bytes 8388624 | tf_op jit(solution)/shard_map/all_gather | solution.py:166
  727.9 6.2 multiply_reduce_fusion.3
  735.0 945.3 %all-gather.19.cloned.1.call-done = bf16[2048,12288]{1,0:T(8,128)(2,1)} async-done(((bf16[256,12288]{1,0:T(8,128)(2,1)}), bf16[2048,12288]{1,0:T(8,128)(2,1)}) %all-gather.19.cloned.1.call-update) | async-done | bytes 50331664 | tf_op jit(solution)/shard_map/all_gather | solution.py:180
  1680.3 13.3 fusion.2
  1693.6 13.2 fusion
  1706.8 456.5 %all-gather.21.cloned.1.call-done = bf16[2048,6144]{1,0:T(8,128)(2,1)} async-done(((bf16[256,6144]{1,0:T(8,128)(2,1)}), bf16[2048,6144]{1,0:T(8,128)(2,1)}) %all-gather.21.cloned.1.call-update) | async-done | bytes 25165840 | tf_op jit(solution)/shard_map/all_gather | solution.py:204
  2163.4 20.1 multiply_convert_fusion
  2183.5 463.0 %all-gather.23.cloned.1.call-done = bf16[2048,6144]{1,0:T(8,128)(2,1)} async-done(((bf16[256,6144]{1,0:T(8,128)(2,1)}), bf16[2048,6144]{1,0:T(8,128)(2,1)}) %all-gather.23.cloned.1.call-update) | async-done | bytes 25165840 | tf_op jit(solution)/shard_map/all_gather | solution.py:222
  2646.5 13.6 fusion.61
  2660.1 469.6 %all-gather.25.cloned.1.call-done = bf16[2048,6144]{1,0:T(8,128)(2,1)} async-done(((bf16[256,6144]{1,0:T(8,128)(2,1)}), bf16[2048,6144]{1,0:T(8,128)(2,1)}) %all-gather.25.cloned.1.call-update) | async-done | bytes 25165840 | tf_op jit(solution)/shard_map/all_gather | solution.py:223
  3129.7 15.2 multiply_reduce_fusion
  3145.0 2.4 multiply_add_fusion.1
  3147.4 8.5 multiply_convert_fusion.3
  3156.5 14.6 fusion.4
  3173.5 10.2 fusion.6
  3183.7 7.7 fusion.9
  3192.7 7.5 bitcast_convert_fusion
  3200.3 4.1 copy.117
  3204.4 4.7 convolution_multiply_fusion
  3210.3 2.6 copy.119
  3212.9 2.5 copy.118
  3215.4 2.2 multiply_add_fusion
  3217.7 2.1 multiply_reduce_fusion.1
  3221.0 4.8 fusion.26
  3225.8 5.7 convolution_convert_fusion.4
  3231.5 5.2 reduce-scatter.5.cloned.1.call-done
  3236.7 1.9 fusion.59
  3239.1 2.5 copy.120
  3243.0 1.6 multiply_reduce_fusion.5
  3245.3 2.7 fusion.38
  3248.0 34.2 reduce-scatter.7.cloned.1.call-done
  3282.2 12.6 convolution_convert_fusion.3
  3294.8 22.6 pad_maximum_fusion.1
  3318.7 13.9 convolution_convert_fusion.1
  3332.6 14.0 convolution_convert_fusion.2
  3346.6 14.2 convolution_convert_fusion
  3360.8 50.7 pad_maximum_fusion
  3411.6 448.8 %reduce-scatter.9.cloned.1.call-done = bf16[256,8192]{1,0:T(8,128)(2,1)} async-done(((bf16[2048,8192]{1,0:T(8,128)(2,1)}), bf16[256,8192]{1,0:T(8,128)(2,1)}) %reduce-scatter.9.cloned.1.call-update) | async-done | bytes 4194320 | tf_op jit(solution)/shard_map/reduce_scatter | solution.py:326
  3860.4 1180.6 %reduce-scatter.11.cloned.1.call-done = bf16[256,18432]{1,0:T(8,128)(2,1)} async-done(((bf16[2048,18432]{1,0:T(8,128)(2,1)}), bf16[256,18432]{1,0:T(8,128)(2,1)}) %reduce-scatter.11.cloned.1.call-update) | async-done | bytes 9437200 | tf_op jit(solution)/shard_map/reduce_scatter | solution.py:230
  5042.5 15.0 fusion.14
  5057.6 14.9 fusion.21
  5072.4 40.8 all-reduce
  5114.5 3.2 fusion.20
  5117.7 164.6 %all-reduce.4.cloned.1.call-done = (bf16[256,8192]{1,0:T(8,128)(2,1)}, bf16[256,18432]{1,0:T(8,128)(2,1)}) async-done(((bf16[256,8192]{1,0:T(8,128)(2,1)}, bf16[256,18432]{1,0:T(8,128)(2,1)}), (bf16[256,8192]{1,0:T(8,128)(2,1)}, bf16[256,18432]{1,0:T(8,128)(2,1)})) %all-reduce.4.cloned.1.call-update) | async-done | bytes 13631504 | tf_op jit(solution)/shard_map/psum | solution.py:67
  5282.3 5.9 slice.91
  5288.2 2.8 slice.92
  5291.0 6.9 fusion.57
  (197 shorter events, 31.6 us)
Async XLA Ops:
  7.2 23.2 copy-start.17
  7.2 485.6 %all-gather.11.cloned.1.call-start = ((), (), s32[]{:S(2)}) async-start(), calls=%async_computation.4 | async-start | bytes 28311552 | tf_op jit(solution)/shard_map/all_gather | solution.py:98
  7.9 547.6 %all-gather.13.cloned.1.call-start = ((), (), s32[]{:S(2)}) async-start(), calls=%async_computation.5 | async-start | bytes 2621440 | tf_op jit(solution)/shard_map/all_gather | solution.py:135
  30.4 474.1 %copy-start.38 = (f32[8,1,256]{2,1,0:T(1,128)}, f32[8,1,256]{2,1,0:T(1,128)S(1)}, u32[]{:S(2)}) copy-start(f32[8,1,256]{2,1,0:T(1,128)S(1)} %convert_element_type.136) | copy-start | bytes 24580
  30.7 473.8 %copy-start.40 = (f32[256]{0:T(256)}, f32[256]{0:T(256)S(1)}, u32[]{:S(2)}) copy-start(f32[256]{0:T(256)S(1)} %add_rsqrt_fusion.3) | copy-start | bytes 3076
  492.8 15.4 copy-start.53
  504.5 2.7 copy-start.13
  508.1 94.6 %all-gather.15.cloned.1.call-start = ((), (), s32[]{:S(2)}) async-start(), calls=%async_computation.6 | async-start | bytes 2621440 | tf_op jit(solution)/shard_map/all_gather | solution.py:134
  508.2 3.6 copy-start.45
  508.2 41.0 copy-start.47
  508.8 42.1 copy-start.28
  508.8 42.1 copy-start.30
  511.8 4.4 copy-start.14
  515.6 212.3 %all-gather.17.cloned.1.call-start = ((), (), s32[]{:S(2)}) async-start(), calls=%async_computation.7 | async-start | bytes 9437184 | tf_op jit(solution)/shard_map/all_gather | solution.py:166
  516.1 1164.2 %all-gather.19.cloned.1.call-start = ((), (), s32[]{:S(2)}) async-start(), calls=%async_computation.8 | async-start | bytes 56623104 | tf_op jit(solution)/shard_map/all_gather | solution.py:180
  521.5 1641.9 %all-gather.21.cloned.1.call-start = ((), (), s32[]{:S(2)}) async-start(), calls=%async_computation.9 | async-start | bytes 28311552 | tf_op jit(solution)/shard_map/all_gather | solution.py:204
  522.1 22.8 copy-start.50
  522.1 22.9 copy-start.51
  522.1 2124.4 %all-gather.23.cloned.1.call-start = ((), (), s32[]{:S(2)}) async-start(), calls=%async_computation.10 | async-start | bytes 28311552 | tf_op jit(solution)/shard_map/all_gather | solution.py:222
  522.9 2606.9 %all-gather.25.cloned.1.call-start = ((), (), s32[]{:S(2)}) async-start(), calls=%async_computation.11 | async-start | bytes 28311552 | tf_op jit(solution)/shard_map/all_gather | solution.py:223
  523.6 2713.1 %reduce-scatter.5.cloned.1.call-start = ((), (), s32[]{:S(2)}) async-start(), calls=%async_computation.12 | async-start | bytes 2621440 | tf_op jit(solution)/shard_map/reduce_scatter | solution.py:282
  552.0 50.7 copy-start.15
  552.0 50.7 copy-start.32
  557.7 72.9 %copy-start.7 = (bf16[128,8,8,128]{3,2,1,0:T(8,128)(2,1)}, bf16[128,8,8,128]{3,2,1,0:T(8,128)(2,1)S(1)}, u32[]{:S(2)}) copy-start(bf16[128,8,8,128]{3,2,1,0:T(8,128)(2,1)S(1)} %copy.123) | copy-start | bytes 6291460
  630.6 4.0 copy-start
  636.5 3.9 copy-start.22
  636.5 91.4 %copy-start.18 = (bf16[256,2048]{1,0:T(8,128)(2,1)S(1)}, bf16[256,2048]{1,0:T(8,128)(2,1)}, u32[]{:S(2)}) copy-start(bf16[256,2048]{1,0:T(8,128)(2,1)} %param.12) | copy-start | bytes 3145732
  734.1 2410.9 %copy-start.20 = (f32[256,2048]{1,0:T(8,128)}, f32[256,2048]{1,0:T(8,128)S(1)}, u32[]{:S(2)}) copy-start(f32[256,2048]{1,0:T(8,128)S(1)} %get-tuple-element.54) | copy-start | bytes 6291460
  735.0 958.6 %copy-start.11 = (bf16[256,2048]{1,0:T(8,128)(2,1)}, bf16[256,2048]{1,0:T(8,128)(2,1)S(1)}, u32[]{:S(2)}) copy-start(bf16[256,2048]{1,0:T(8,128)(2,1)S(1)} %multiply_convert_fusion.5) | copy-start | bytes 3145732
  3129.7 15.2 copy-start.24
  3145.0 2.4 copy-start.23
  3147.4 8.5 copy-start.4
  3156.4 14.7 slice-start
  3156.4 14.7 slice-start.1
  3156.5 15.9 slice-start.2
  3156.5 17.0 slice-start.3
  3173.5 10.2 copy-start.16
  3183.7 7.8 copy-start.46
  3183.7 8.4 copy-start.48
  3191.5 90.7 %reduce-scatter.7.cloned.1.call-start = ((), (), s32[]{:S(2)}) async-start(), calls=%async_computation.13 | async-start | bytes 2621440 | tf_op jit(solution)/shard_map/reduce_scatter | solution.py:288
  3200.3 4.2 copy-start.8
  3204.4 656.0 %reduce-scatter.9.cloned.1.call-start = ((), (), s32[]{:S(2)}) async-start(), calls=%async_computation.14 | async-start | bytes 37748736 | tf_op jit(solution)/shard_map/reduce_scatter | solution.py:326
  3210.3 5.1 copy-start.29
  3210.3 5.1 copy-start.31
  3215.4 2.3 copy-start.3
  3215.4 2.3 copy-start.35
  3221.0 4.8 copy-start.5
  3221.0 4.8 copy-start.27
  3225.8 56.4 %copy-start.26 = (bf16[256,2048]{1,0:T(8,128)(2,1)}, bf16[256,2048]{1,0:T(8,128)(2,1)S(1)}, u32[]{:S(2)}) copy-start(bf16[256,2048]{1,0:T(8,128)(2,1)S(1)} %get-tuple-element.27) | copy-start | bytes 3145732
  3239.1 3.9 copy-start.10
  3239.1 3.9 copy-start.37
  3243.0 2.3 copy-start.44
  3244.9 37.3 copy-start.19
  3245.0 37.3 copy-start.39
  3245.0 37.3 copy-start.41
  3248.0 46.8 copy-start.33
  3317.5 1723.4 %reduce-scatter.11.cloned.1.call-start = ((), (), s32[]{:S(2)}) async-start(), calls=%async_computation.15 | async-start | bytes 84934656 | tf_op jit(solution)/shard_map/reduce_scatter | solution.py:230
  3332.6 14.0 copy-start.25
  3411.5 1870.8 %all-reduce.4.cloned.1.call-start = ((), (), s32[]{:S(2)}) async-start(), calls=%async_computation.16 | async-start | bytes 27262976 | tf_op jit(solution)/shard_map/psum | solution.py:67
  5040.9 1.6 copy-start.21
  5042.5 15.0 copy-start.43
  5057.5 14.9 copy-start.49
  5057.5 57.0 %copy-start.6 = (f32[256,2048]{1,0:T(8,128)S(1)}, f32[256,2048]{1,0:T(8,128)}, u32[]{:S(2)}) copy-start(f32[256,2048]{1,0:T(8,128)} %copy-done.4) | copy-start | bytes 6291460
  5282.3 8.7 copy-start.1
  (8 other events, 9.0 us)
Sparse Core Ops, SparseCore 0:
  9.6 483.1 all-gather.10
  508.2 47.2 all-gather.12
  557.7 44.9 all-gather.14
  604.6 123.1 all-gather.16
  729.8 950.4 all-gather.18
  1681.7 481.6 all-gather.20
  2164.9 481.6 all-gather.22
  2648.1 481.6 all-gather.24
  3191.6 45.0 reduce-scatter.4
  3239.0 43.2 reduce-scatter.6
  3317.6 542.6 reduce-scatter.8
  3864.1 1176.8 reduce-scatter.10
  5043.7 238.5 all-reduce.3
